TPU v7x, 32 devices: a whole 2x2x4 slice. The times are simulated.
32 devices in a mesh: head: 4 (over z), blk: 8 (over y, x, core).
Axes of the slice: x: 2, y: 2, z: 4, core: 2. Of those that a mesh axis runs over, the one named last changes fastest.
Arguments:
- tokens: bfloat16 [8192, 1024], P(('blk', 'head')), may hold values from -6 to 6
- cotangent: bfloat16 [8192, 1024], P(('blk', 'head')), may hold values from -6 to 6
- segment: int32 [8192], replicated, may hold values from 0 to 3, never falling along the last dimension, each value on 1 to 6144 neighbouring positions
- norm_gain: bfloat16 [1024], P(('head', 'blk')), may hold values from 0.5 to 1.5
- norm_shift: bfloat16 [1024], P(('head', 'blk')), may hold values from -1.5 to 1.5
- in_weight: bfloat16 [1024, 3072], P(('head', 'blk')), may hold values from -0.1875 to 0.1875
- query_bias: bfloat16 [1024], P(('head', 'blk')), may hold values from -2.5 to 2.5
- value_bias: bfloat16 [1024], P(('head', 'blk')), may hold values from -1.5 to 1.5
- out_weight: bfloat16 [1024, 1024], P(('head', 'blk')), may hold values from -3 to 3
- out_bias: bfloat16 [1024], P(('head', 'blk')), may hold values from -1.5 to 1.5
- post_gain: bfloat16 [1024], P(('head', 'blk')), may hold values from 0.5 to 1.5
- post_shift: bfloat16 [1024], P(('head', 'blk')), may hold values from -1.5 to 1.5
- up_weight: bfloat16 [1024, 4096], P(('head', 'blk')), may hold values from -0.1875 to 0.1875
- up_bias: bfloat16 [4096], P(('head', 'blk')), may hold values from -1.5 to 1.5
- down_weight: bfloat16 [4096, 1024], P(('head', 'blk')), may hold values from -0.09375 to 0.09375
- down_bias: bfloat16 [1024], P(('head', 'blk')), may hold values from -1.5 to 1.5
Outputs:
- output: bfloat16 [8192, 1024], P(('blk', 'head'))
- tokens_grad: bfloat16 [8192, 1024], P(('blk', 'head'))
- norm_gain_grad: float32 [1024], P(('head', 'blk'))
- norm_shift_grad: float32 [1024], P(('head', 'blk'))
- in_weight_grad: float32 [1024, 3072], P(('head', 'blk'))
- query_bias_grad: float32 [1024], P(('head', 'blk'))
- value_bias_grad: float32 [1024], P(('head', 'blk'))
- out_weight_grad: float32 [1024, 1024], P(('head', 'blk'))
- out_bias_grad: float32 [1024], P(('head', 'blk'))
- post_gain_grad: float32 [1024], P(('head', 'blk'))
- post_shift_grad: float32 [1024], P(('head', 'blk'))
- up_weight_grad: float32 [1024, 4096], P(('head', 'blk'))
- up_bias_grad: float32 [4096], P(('head', 'blk'))
- down_weight_grad: float32 [4096, 1024], P(('head', 'blk'))
- down_bias_grad: float32 [1024], P(('head', 'blk'))
Inputs may be any that keep to these rules, and one draw needn't show every extreme that they name: `segment`: document numbers never fall along the sequence; each document holds 1 to 6144 tokens and one holds exactly 6144.
All inputs are finite; a program needn't handle non-finite values.
Results may differ from a plain program's by a relative error of at most 0.019.
Values may be sent and summed in bfloat16 or wider, within the bound.
No kernel may reach another device: no remote copies, remote signals or barrier semaphores. Data moves between devices by JAX's collectives and lax.ppermute only.
A program may use at most 256 MiB of HBM per device.

v0:
```python
import jax
import jax.numpy as jnp
from jax import lax
from jax.sharding import PartitionSpec as P

HEADS = 16
HEAD_DIM = 64
EPS = 1e-05
NEGATIVE = -1e30
GELU_C = 0.7978845608028654


def norm_forward(rows, gain, shift):
    center = rows - jnp.mean(rows, axis=-1, keepdims=True)
    var = jnp.mean(center * center, axis=-1, keepdims=True)
    inverse = lax.rsqrt(var + EPS)
    unit = center * inverse
    return (unit * gain + shift, unit, inverse)


def norm_backward(grad, unit, inverse, gain):
    scaled = grad * gain
    inner = (
        scaled
        - jnp.mean(scaled, axis=-1, keepdims=True)
        - unit * jnp.mean(scaled * unit, axis=-1, keepdims=True)
    )
    return (inverse * inner, jnp.sum(grad * unit, axis=0), jnp.sum(grad, axis=0))


def gelu_parts(pre):
    cubic = pre * pre * pre
    tangent = jnp.tanh(GELU_C * (pre + 0.044715 * cubic))
    value = 0.5 * pre * (1.0 + tangent)
    slope = 0.5 * (1.0 + tangent) + 0.5 * pre * (1.0 - tangent * tangent) * GELU_C * (
        1.0 + 3.0 * 0.044715 * pre * pre
    )
    return (value, slope)


def on_device(
    tokens,
    cotangent,
    segment,
    norm_gain,
    norm_shift,
    in_weight,
    query_bias,
    value_bias,
    out_weight,
    out_bias,
    post_gain,
    post_shift,
    up_weight,
    up_bias,
    down_weight,
    down_bias,
):
    n_head = lax.axis_size("head")
    n_blk = lax.axis_size("blk")
    group = lax.axis_index("blk")
    tok_rows = tokens.shape[0]
    width = tokens.shape[1]
    block_rows = tok_rows * n_head
    head_group = HEADS // n_head
    group_width = head_group * HEAD_DIM
    scale = HEAD_DIM ** (-0.5)
    q_first = group * block_rows
    f32 = jnp.float32
    bf16 = jnp.bfloat16
    gain_a, shift_a, w_in, bias_q, bias_v, w_out, bias_out = (
        lax.all_gather(norm_gain, ("head", "blk"), axis=0, tiled=True),
        lax.all_gather(norm_shift, ("head", "blk"), axis=0, tiled=True),
        lax.all_gather(in_weight, ("head", "blk"), axis=0, tiled=True),
        lax.all_gather(query_bias, ("head", "blk"), axis=0, tiled=True),
        lax.all_gather(value_bias, ("head", "blk"), axis=0, tiled=True),
        lax.all_gather(out_weight, ("head", "blk"), axis=0, tiled=True),
        lax.all_gather(out_bias, ("head", "blk"), axis=0, tiled=True),
    )
    rows = tokens.astype(f32)
    normed, unit_in, inverse_in = norm_forward(rows, gain_a.astype(f32), shift_a.astype(f32))
    normed_low = normed.astype(bf16)
    bias_full = jnp.concatenate([bias_q, jnp.zeros((width,), bf16), bias_v]).astype(f32)
    projected = (jnp.dot(normed_low, w_in, preferred_element_type=f32) + bias_full).astype(bf16)
    grouped = lax.all_to_all(
        projected.reshape(tok_rows, 3, n_head, group_width),
        "head",
        split_axis=2,
        concat_axis=0,
        tiled=True,
    )
    grouped = grouped.reshape(block_rows, 3, head_group, HEAD_DIM)
    queries = grouped[:, 0]
    kv_local = grouped[:, 1:].reshape(block_rows, 2, group_width)
    seg_query = lax.dynamic_slice_in_dim(segment, q_first, block_rows)
    first_doc = seg_query[0]
    query_pos = q_first + lax.iota(jnp.int32, block_rows)

    def block_scores(keys, key_start):
        key_pos = key_start + lax.iota(jnp.int32, block_rows)
        seg_key = lax.dynamic_slice_in_dim(segment, key_start, block_rows)
        allowed = (key_pos[None, :] <= query_pos[:, None]) & (
            seg_key[None, :] == seg_query[:, None]
        )
        scores = jnp.einsum("qhd,khd->hqk", queries, keys, preferred_element_type=f32) * scale
        return (scores, allowed[None])

    def visible(key_start):
        last_doc = lax.dynamic_index_in_dim(segment, key_start + block_rows - 1, keepdims=False)
        return (key_start <= q_first + block_rows - 1) & (last_doc >= first_doc)

    def split_pair(block):
        pair = block.reshape(block_rows, 2, head_group, HEAD_DIM)
        return (pair[:, 0], pair[:, 1])

    start_state = (
        jnp.zeros((block_rows, head_group, HEAD_DIM), f32),
        jnp.full((head_group, block_rows), NEGATIVE, f32),
        jnp.zeros((head_group, block_rows), f32),
    )
    piece = lax.all_gather(kv_local, "blk", axis=0, tiled=True)
    count = piece.shape[0] // block_rows
    blocks = piece.reshape(count, block_rows, 2, group_width)

    def forward_advance(state, item):
        block, index = item
        key_start = index * block_rows

        def forward_update(inner):
            acc, run_max, run_sum = inner
            keys, values = split_pair(block)
            scores, allowed = block_scores(keys, key_start)
            new_max = jnp.maximum(run_max, jnp.max(jnp.where(allowed, scores, NEGATIVE), axis=2))
            weights = jnp.where(allowed, jnp.exp(scores - new_max[:, :, None]), 0.0)
            factor = jnp.exp(run_max - new_max)
            new_sum = run_sum * factor + jnp.sum(weights, axis=2)
            mixed = jnp.einsum(
                "hqk,khd->qhd", weights.astype(bf16), values, preferred_element_type=f32
            )
            return (acc * factor.T[:, :, None] + mixed, new_max, new_sum)

        return (lax.cond(visible(key_start), forward_update, lambda inner: inner, state), None)

    state, _ = lax.scan(forward_advance, start_state, (blocks, jnp.arange(count, dtype=jnp.int32)))
    acc, run_max, run_sum = state
    attended = acc / run_sum.T[:, :, None]
    log_total = run_max + jnp.log(run_sum)
    attended_low = attended.astype(bf16)
    back_rows = lax.all_to_all(
        attended_low.reshape(block_rows, 1, group_width),
        "head",
        split_axis=0,
        concat_axis=1,
        tiled=True,
    )
    back_rows = back_rows.reshape(tok_rows, width)
    branch = jnp.dot(back_rows, w_out, preferred_element_type=f32) + bias_out.astype(f32)
    middle = rows + branch
    gain_b, shift_b, w_up, bias_up, w_down, bias_down = (
        lax.all_gather(post_gain, ("head", "blk"), axis=0, tiled=True),
        lax.all_gather(post_shift, ("head", "blk"), axis=0, tiled=True),
        lax.all_gather(up_weight, ("head", "blk"), axis=0, tiled=True),
        lax.all_gather(up_bias, ("head", "blk"), axis=0, tiled=True),
        lax.all_gather(down_weight, ("head", "blk"), axis=0, tiled=True),
        lax.all_gather(down_bias, ("head", "blk"), axis=0, tiled=True),
    )
    hidden_in, unit_mid, inverse_mid = norm_forward(middle, gain_b.astype(f32), shift_b.astype(f32))
    hidden_low = hidden_in.astype(bf16)
    pre = jnp.dot(hidden_low, w_up, preferred_element_type=f32) + bias_up.astype(f32)
    act, slope = gelu_parts(pre)
    act_low = act.astype(bf16)
    result = middle + jnp.dot(act_low, w_down, preferred_element_type=f32) + bias_down.astype(f32)
    output = result.astype(bf16)
    grad_out = cotangent.astype(f32)
    down_bias_grad = jnp.sum(grad_out, axis=0)
    down_weight_grad = jnp.einsum("tf,td->fd", act_low, cotangent, preferred_element_type=f32)
    grad_act = jnp.einsum("td,fd->tf", cotangent, w_down, preferred_element_type=f32)
    grad_pre = (grad_act * slope).astype(bf16)
    up_bias_grad = jnp.sum(grad_pre.astype(f32), axis=0)
    up_weight_grad = jnp.einsum("td,tf->df", hidden_low, grad_pre, preferred_element_type=f32)
    grad_hidden = jnp.einsum("tf,df->td", grad_pre, w_up, preferred_element_type=f32)
    grad_mid_in, post_gain_grad, post_shift_grad = norm_backward(
        grad_hidden, unit_mid, inverse_mid, gain_b.astype(f32)
    )
    grad_middle = grad_out + grad_mid_in
    (
        post_gain_grad,
        post_shift_grad,
        up_weight_grad,
        up_bias_grad,
        down_weight_grad,
        down_bias_grad,
    ) = (
        lax.psum_scatter(post_gain_grad, ("head", "blk"), scatter_dimension=0, tiled=True),
        lax.psum_scatter(post_shift_grad, ("head", "blk"), scatter_dimension=0, tiled=True),
        lax.psum_scatter(up_weight_grad, ("head", "blk"), scatter_dimension=0, tiled=True),
        lax.psum_scatter(up_bias_grad, ("head", "blk"), scatter_dimension=0, tiled=True),
        lax.psum_scatter(down_weight_grad, ("head", "blk"), scatter_dimension=0, tiled=True),
        lax.psum_scatter(down_bias_grad, ("head", "blk"), scatter_dimension=0, tiled=True),
    )
    grad_branch = grad_middle.astype(bf16)
    out_bias_grad = jnp.sum(grad_branch.astype(f32), axis=0)
    out_weight_grad = jnp.einsum("td,te->de", back_rows, grad_branch, preferred_element_type=f32)
    grad_back = jnp.einsum("te,de->td", grad_branch, w_out, preferred_element_type=f32).astype(bf16)
    grad_heads = lax.all_to_all(
        grad_back.reshape(tok_rows, n_head, group_width),
        "head",
        split_axis=1,
        concat_axis=0,
        tiled=True,
    )
    grad_heads = grad_heads.reshape(block_rows, head_group, HEAD_DIM)
    delta = jnp.sum(grad_heads.astype(f32) * attended, axis=-1).T

    def block_backward(block, key_start):
        keys, values = split_pair(block)
        scores, allowed = block_scores(keys, key_start)
        probs = jnp.where(allowed, jnp.exp(scores - log_total[:, :, None]), 0.0)
        grad_probs = jnp.einsum("qhd,khd->hqk", grad_heads, values, preferred_element_type=f32)
        grad_scores = (probs * (grad_probs - delta[:, :, None])).astype(bf16)
        grad_values = jnp.einsum(
            "hqk,qhd->khd", probs.astype(bf16), grad_heads, preferred_element_type=f32
        )
        grad_keys = (
            jnp.einsum("hqk,qhd->khd", grad_scores, queries, preferred_element_type=f32) * scale
        )
        query_add = (
            jnp.einsum("hqk,khd->qhd", grad_scores, keys, preferred_element_type=f32) * scale
        )
        return (query_add, jnp.stack([grad_keys, grad_values], axis=1))

    back_state = (
        jnp.zeros((block_rows, head_group, HEAD_DIM), f32),
        jnp.zeros((block_rows * n_blk, 2, head_group, HEAD_DIM), f32),
    )
    piece = lax.all_gather(kv_local, "blk", axis=0, tiled=True)
    count = piece.shape[0] // block_rows
    blocks = piece.reshape(count, block_rows, 2, group_width)

    def backward_advance(state, item):
        block, index = item
        key_start = index * block_rows

        def backward_update(inner):
            grad_query, grad_pairs = inner
            query_add, pair_add = block_backward(block, key_start)
            current = lax.dynamic_slice_in_dim(grad_pairs, key_start, block_rows, 0)
            return (
                grad_query + query_add,
                lax.dynamic_update_slice_in_dim(grad_pairs, current + pair_add, key_start, 0),
            )

        return (lax.cond(visible(key_start), backward_update, lambda inner: inner, state), None)

    state, _ = lax.scan(backward_advance, back_state, (blocks, jnp.arange(count, dtype=jnp.int32)))
    grad_query, grad_pairs = state
    pair_sums = lax.psum_scatter(
        grad_pairs.reshape(block_rows * n_blk, 2, group_width).astype(jnp.bfloat16),
        "blk",
        scatter_dimension=0,
        tiled=True,
    ).astype(jnp.float32)
    grad_joint = jnp.concatenate(
        [grad_query.reshape(block_rows, 1, group_width).astype(bf16), pair_sums.astype(bf16)],
        axis=1,
    )
    grad_rows = lax.all_to_all(
        grad_joint.reshape(block_rows, 3, 1, group_width),
        "head",
        split_axis=0,
        concat_axis=2,
        tiled=True,
    )
    grad_proj = grad_rows.reshape(tok_rows, 3 * width)
    query_bias_grad = jnp.sum(grad_proj[:, :width].astype(f32), axis=0)
    value_bias_grad = jnp.sum(grad_proj[:, 2 * width :].astype(f32), axis=0)
    in_weight_grad = jnp.einsum("td,te->de", normed_low, grad_proj, preferred_element_type=f32)
    grad_normed = jnp.einsum("te,de->td", grad_proj, w_in, preferred_element_type=f32)
    grad_rows_in, norm_gain_grad, norm_shift_grad = norm_backward(
        grad_normed, unit_in, inverse_in, gain_a.astype(f32)
    )
    tokens_grad = (grad_middle + grad_rows_in).astype(bf16)
    (
        norm_gain_grad,
        norm_shift_grad,
        in_weight_grad,
        query_bias_grad,
        value_bias_grad,
        out_weight_grad,
        out_bias_grad,
    ) = (
        lax.psum_scatter(norm_gain_grad, ("head", "blk"), scatter_dimension=0, tiled=True),
        lax.psum_scatter(norm_shift_grad, ("head", "blk"), scatter_dimension=0, tiled=True),
        lax.psum_scatter(in_weight_grad, ("head", "blk"), scatter_dimension=0, tiled=True),
        lax.psum_scatter(query_bias_grad, ("head", "blk"), scatter_dimension=0, tiled=True),
        lax.psum_scatter(value_bias_grad, ("head", "blk"), scatter_dimension=0, tiled=True),
        lax.psum_scatter(out_weight_grad, ("head", "blk"), scatter_dimension=0, tiled=True),
        lax.psum_scatter(out_bias_grad, ("head", "blk"), scatter_dimension=0, tiled=True),
    )
    return (
        output,
        tokens_grad,
        norm_gain_grad,
        norm_shift_grad,
        in_weight_grad,
        query_bias_grad,
        value_bias_grad,
        out_weight_grad,
        out_bias_grad,
        post_gain_grad,
        post_shift_grad,
        up_weight_grad,
        up_bias_grad,
        down_weight_grad,
        down_bias_grad,
    )


def solution(mesh):
    placed = (
        P(("blk", "head"), None),
        P(("blk", "head"), None),
        P(),
        P(("head", "blk")),
        P(("head", "blk")),
        P(("head", "blk"), None),
        P(("head", "blk")),
        P(("head", "blk")),
        P(("head", "blk"), None),
        P(("head", "blk")),
        P(("head", "blk")),
        P(("head", "blk")),
        P(("head", "blk"), None),
        P(("head", "blk")),
        P(("head", "blk"), None),
        P(("head", "blk")),
    )
    return jax.shard_map(
        on_device,
        mesh=mesh,
        in_specs=placed,
        out_specs=(
            P(("blk", "head"), None),
            P(("blk", "head"), None),
            P(("head", "blk")),
            P(("head", "blk")),
            P(("head", "blk"), None),
            P(("head", "blk")),
            P(("head", "blk")),
            P(("head", "blk"), None),
            P(("head", "blk")),
            P(("head", "blk")),
            P(("head", "blk")),
            P(("head", "blk"), None),
            P(("head", "blk")),
            P(("head", "blk"), None),
            P(("head", "blk")),
        ),
        check_vma=False,
    )
```

profile of v0, /device:TPU:14, one launch (start us, length us, event | category | flops | bytes accessed | tf_op | source)
XLA Modules:
  0.0 1566.0 jit_solution(17215553345524749497)
XLA Ops:
  14.7 41.5 %all-reduce.18 = (bf16[1024]{0:T(1024)(128)(2,1)S(1)}, bf16[1024]{0:T(1024)(128)(2,1)S(1)}, bf16[1024]{0:T(1024)(128)(2,1)S(1)}, bf16[1024]{0:T(1024)(128)(2,1)S...) all-reduce(bf16[1024]{0:T(1024)(128)(2,1)S(1)} %dynamic-update-slic, ...), channel_id=1, replica_groups=mesh['head'=4,'blk'=8] {'head','blk'}, use_global_device_ids=true, to_apply=%add.3 | all-reduce | flops 8192 | bytes 32768
  59.0 21.8 %all-gather.7.cloned.1.call-done = bf16[1024,3072]{1,0:T(8,128)(2,1)} async-done(((bf16[32,3072]{1,0:T(8,128)(2,1)}), bf16[1024,3072]{1,0:T(8,128)(2,1)}) %all-gather.7.cloned.1.call-update) | async-done | bytes 6291472 | tf_op jit(solution)/shard_map/all_gather | solution.py:74
  90.3 39.0 %all_to_all.60 = bf16[256,3,4,256]{3,0,1,2:T(8,128)(2,1)S(1)} all-to-all(bf16[256,3,4,256]{3,0,1,2:T(8,128)(2,1)S(1)} %copy.93), channel_id=1, replica_groups=mesh['head'=4,'blk'=8] {'head'}, dimensions={2} | all-to-all | bytes 3145728 | tf_op jit(solution)/shard_map/all_to_all | solution.py:85
  138.6 50.8 %all-gather.9.cloned.1.call-done = bf16[8192,2,256]{0,2,1:T(8,128)(2,1)} async-done(((bf16[1024,2,256]{0,2,1:T(8,128)(2,1)}), bf16[8192,2,256]{0,2,1:T(8,128)(2,1)}) %all-gather.9.cloned.1.call-update) | async-done | bytes 8388624 | tf_op jit(solution)/shard_map/all_gather | solution.py:121
  189.4 12.0 copy.95
  201.4 11.5 copy.96
  213.1 45.0 %while.38 = (s32[]{:T(128)}, f32[1024,4,64]{0,2,1:T(8,128)S(1)}, f32[4,1024]{1,0:T(4,128)S(1)}, f32[4,1024]{1,0:T(4,128)S(1)}, s32[8]{0:T(128)S(1)}, /*index=5*/...) while((s32[]{:T(128)}, f32[1024,4,64]{0,2,1:T(8,128)S(1)}, ...), condition=%wide.region_7.8_spmd.clone, body=%wide.region_2.7_spmd.clone.sunk | while | flops 1123563520 | bytes 60596688 | solution.py:144
  240.2 13.9 conditional.6
  266.1 95.4 %all-gather = bf16[32,1,128]{2,1,0:T(2,128)(2,1)S(1)} all-gather(bf16[1,1,128]{2,1,0:T(2,128)(2,1)S(1)} %bitcast.161), channel_id=1, replica_groups=mesh['head'=4,'blk'=8] {'head','blk'}, dimensions={0}, use_global_device_ids=true | all-gather | bytes 8448 | tf_op jit(solution)/shard_map/all_gather | solution.py:163
  377.8 39.5 %all-gather.15.cloned.1.call-done = bf16[4096,1024]{1,0:T(8,128)(2,1)} async-done(((bf16[128,1024]{1,0:T(8,128)(2,1)}), bf16[4096,1024]{1,0:T(8,128)(2,1)}) %all-gather.15.cloned.1.call-update) | async-done | bytes 8388624 | tf_op jit(solution)/shard_map/all_gather | solution.py:164
  417.3 11.8 convert_reduce_fusion
  440.0 12.0 all-to-all-done.2
  463.7 81.5 %while.39 = (s32[]{:T(128)}, f32[1024,4,64]{0,2,1:T(8,128)}, f32[8192,2,4,64]{0,3,2,1:T(8,128)}, s32[8]{0:T(128)S(1)}, s32[]{:T(128)}, /*index=5*/s32[8192]{0:T(...) while((s32[]{:T(128)}, f32[1024,4,64]{0,2,1:T(8,128)}, ...), condition=%wide.region_16.17_spmd.clone, body=%wide.region_13.16_spmd.clone.sunk | while | flops 2731280384 | bytes 103375360 | solution.py:255
  490.9 50.1 %conditional.7 = ((f32[1024,4,64]{0,2,1:T(8,128)}, f32[8192,2,4,64]{0,3,2,1:T(8,128)})) conditional(s32[]{:T(128)} %convert_element_type.245, (f32[1024,4,64]{0,2,1:T(8,128)}, f32[8192,2,4,64]{0,3,2,1:T(8,128)}) %tuple.143, (s32[]{:T(128)}, s32[]{:T(128)}, s32[8192]{0:T(1024)}, s32[1024]{0:T(1024)S(1)}, bf16[8,1024,2,256]{1,3,2,0:T(8,128)(2,1)}, ...), branch_computations={%region_14.14_spmd, %region_15.15_spmd} | conditional | flops 2731280384 | bytes 103370856 | solution.py:253
  502.3 10.3 fusion.27
  530.6 10.4 dynamic_update_slice.3
  559.5 316.2 %reduce-scatter.6.cloned.1.call-done = bf16[1024,2,256]{0,2,1:T(8,128)(2,1)} async-done(((bf16[8192,2,256]{0,2,1:T(8,128)(2,1)}), bf16[1024,2,256]{0,2,1:T(8,128)(2,1)}) %reduce-scatter.6.cloned.1.call-update) | async-done | bytes 1048592 | tf_op jit(solution)/shard_map/reduce_scatter | solution.py:257
  882.3 59.2 %all_to_all.61 = bf16[1024,3,1,256]{3,1,2,0:T(4,128)(2,1)S(1)} all-to-all(bf16[1024,3,1,256]{3,1,2,0:T(4,128)(2,1)} %copy.102), channel_id=1, replica_groups=mesh['head'=4,'blk'=8] {'head'}, dimensions={0} | all-to-all | bytes 3145728 | tf_op jit(solution)/shard_map/all_to_all | solution.py:267
  954.6 10.8 fusion.70
  966.6 9.8 fusion.69
  991.0 41.1 %all-reduce.17 = (f32[1024]{0:T(1024)S(1)}, f32[1024]{0:T(1024)S(1)}, f32[1024]{0:T(1024)S(1)}, f32[1024]{0:T(1024)S(1)}, f32[1024]{0:T(1024)S(1)}, /*index=5*/f...) all-reduce(f32[1024]{0:T(1024)S(1)} %get-tuple-element.973, ...), channel_id=3, replica_groups=mesh['head'=4,'blk'=8] {'head','blk'}, use_global_device_ids=true, to_apply=%region_21.22.clone | all-reduce | flops 12288 | bytes 98304
  1038.5 145.6 %reduce-scatter.8.cloned.1.call-done = f32[32,3072]{1,0:T(8,128)} async-done(((f32[1024,3072]{1,0:T(8,128)}), f32[32,3072]{1,0:T(8,128)}) %reduce-scatter.8.cloned.1.call-update) | async-done | bytes 393232 | tf_op jit(solution)/shard_map/reduce_scatter | solution.py:294
  1184.1 187.4 %reduce-scatter.14.cloned.1.call-done = f32[128,1024]{1,0:T(8,128)} async-done(((f32[4096,1024]{1,0:T(8,128)}), f32[128,1024]{1,0:T(8,128)}) %reduce-scatter.14.cloned.1.call-update) | async-done | bytes 524304 | tf_op jit(solution)/shard_map/reduce_scatter | solution.py:198
  1371.5 187.2 %reduce-scatter.12.cloned.1.call-done = f32[32,4096]{1,0:T(8,128)} async-done(((f32[1024,4096]{1,0:T(8,128)}), f32[32,4096]{1,0:T(8,128)}) %reduce-scatter.12.cloned.1.call-update) | async-done | bytes 524304 | tf_op jit(solution)/shard_map/reduce_scatter | solution.py:196
  (271 shorter events, 205.0 us)
Async XLA Ops:
  7.2 73.5 %all-gather.7.cloned.1.call-start = ((), (), s32[]{:S(2)}) async-start(), calls=%async_computation.9 | async-start | bytes 6488064 | tf_op jit(solution)/shard_map/all_gather | solution.py:74
  7.9 181.5 %all-gather.9.cloned.1.call-start = ((), (), s32[]{:S(2)}) async-start(), calls=%async_computation.10 | async-start | bytes 9437184 | tf_op jit(solution)/shard_map/all_gather | solution.py:121
  56.2 30.6 %copy-start.17 = (f32[1024]{0:T(1024)}, f32[1024]{0:T(1024)S(1)}, u32[]{:S(2)}) copy-start(f32[1024]{0:T(1024)S(1)} %convert_element_type.136) | copy-start | bytes 12292
  56.2 30.5 %copy-start.19 = (f32[1024]{0:T(1024)}, f32[1024]{0:T(1024)S(1)}, u32[]{:S(2)}) copy-start(f32[1024]{0:T(1024)S(1)} %convert_element_type.137) | copy-start | bytes 12292
  57.4 29.3 %copy-start.23 = (f32[256]{0:T(256)}, f32[256]{0:T(256)S(1)}, u32[]{:S(2)}) copy-start(f32[256]{0:T(256)S(1)} %broadcast_multiply_fusion.5) | copy-start | bytes 3076
  58.9 27.8 %copy-start.27 = (f32[256]{0:T(256)}, f32[256]{0:T(256)S(1)}, u32[]{:S(2)}) copy-start(f32[256]{0:T(256)S(1)} %add_rsqrt_fusion.1) | copy-start | bytes 3076
  135.4 231.2 %all-gather.11.cloned.1.call-start = ((), (), s32[]{:S(2)}) async-start(), calls=%async_computation.11 | async-start | bytes 2162688 | tf_op jit(solution)/shard_map/all_gather | solution.py:77
  136.2 233.6 %all-gather.13.cloned.1.call-start = ((), (), s32[]{:S(2)}) async-start(), calls=%async_computation.12 | async-start | bytes 8650752 | tf_op jit(solution)/shard_map/all_gather | solution.py:162
  136.7 280.6 %all-gather.15.cloned.1.call-start = ((), (), s32[]{:S(2)}) async-start(), calls=%async_computation.13 | async-start | bytes 8650752 | tf_op jit(solution)/shard_map/all_gather | solution.py:164
  258.7 108.0 %copy-start.5 = (bf16[256,1024]{1,0:T(8,128)(2,1)S(1)}, bf16[256,1024]{1,0:T(8,128)(2,1)}, u32[]{:S(2)}) copy-start(bf16[256,1024]{1,0:T(8,128)(2,1)} %param.24) | copy-start | bytes 1572868
  260.9 100.6 %all-to-all-start.1 = ((bf16[4,2,32768]{2,1,0:T(2,128)(2,1)}), bf16[4,2,32768]{2,1,0:T(2,128)(2,1)}, u32[]{:S(2)}, u32[]{:S(2)}) async-start(bf16[4,2,32768]{2,1,0:T(2,128)(2,1)} %reshape.311), calls=%async_computation.1 | async-start | bytes 1048576 | tf_op jit(solution)/shard_map/all_to_all | solution.py:149
  266.0 166.3 %copy-start.13 = (f32[1024]{0:T(1024)}, f32[1024]{0:T(1024)S(1)}, u32[]{:S(2)}) copy-start(f32[1024]{0:T(1024)S(1)} %convert_element_type.143) | copy-start | bytes 12292
  266.1 103.7 %copy-start.15 = (f32[1024]{0:T(1024)}, f32[1024]{0:T(1024)S(1)}, u32[]{:S(2)}) copy-start(f32[1024]{0:T(1024)S(1)} %convert_element_type.144) | copy-start | bytes 12292
  369.5 62.9 %copy-start.1 = (f32[256,1024]{1,0:T(8,128)}, f32[256,1024]{1,0:T(8,128)S(1)}, u32[]{:S(2)}) copy-start(f32[256,1024]{1,0:T(8,128)S(1)} %get-tuple-element.1062) | copy-start | bytes 3145732
  369.5 62.9 %copy-start.21 = (f32[256]{0:T(256)}, f32[256]{0:T(256)S(1)}, u32[]{:S(2)}) copy-start(f32[256]{0:T(256)S(1)} %broadcast_multiply_fusion.4) | copy-start | bytes 3076
  369.8 62.6 %copy-start.25 = (f32[256]{0:T(256)}, f32[256]{0:T(256)S(1)}, u32[]{:S(2)}) copy-start(f32[256]{0:T(256)S(1)} %add_rsqrt_fusion) | copy-start | bytes 3076
  369.8 47.5 %copy-start.10 = (bf16[256,1024]{1,0:T(8,128)(2,1)S(1)}, bf16[256,1024]{1,0:T(8,128)(2,1)}, u32[]{:S(2)}) copy-start(bf16[256,1024]{1,0:T(8,128)(2,1)} %param.25) | copy-start | bytes 1572868
  417.3 11.8 copy-start.36
  436.1 15.9 %all-to-all-start.2 = ((bf16[256,4,256]{2,0,1:T(8,128)(2,1)}), bf16[256,4,256]{2,0,1:T(8,128)(2,1)S(1)}, u32[]{:S(2)}, u32[]{:S(2)}) async-start(bf16[256,4,256]{2,0,1:T(8,128)(2,1)} %bitcast.128), calls=%async_computation.2 | async-start | bytes 1048576 | tf_op jit(solution)/shard_map/all_to_all | solution.py:205
  440.0 435.7 %reduce-scatter.6.cloned.1.call-start = ((), (), s32[]{:S(2)}) async-start(), calls=%async_computation.14 | async-start | bytes 9437184 | tf_op jit(solution)/shard_map/reduce_scatter | solution.py:257
  554.1 484.4 %reduce-scatter.10.cloned.1.call-start = ((), (), s32[]{:S(2)}) async-start(), calls=%async_computation.16 | async-start | bytes 4325376 | tf_op jit(solution)/shard_map/reduce_scatter | solution.py:297
  558.1 626.0 %reduce-scatter.8.cloned.1.call-start = ((), (), s32[]{:S(2)}) async-start(), calls=%async_computation.15 | async-start | bytes 12976128 | tf_op jit(solution)/shard_map/reduce_scatter | solution.py:294
  953.5 418.0 %reduce-scatter.14.cloned.1.call-start = ((), (), s32[]{:S(2)}) async-start(), calls=%async_computation.18 | async-start | bytes 17301504 | tf_op jit(solution)/shard_map/reduce_scatter | solution.py:198
  965.4 593.3 %reduce-scatter.12.cloned.1.call-start = ((), (), s32[]{:S(2)}) async-start(), calls=%async_computation.17 | async-start | bytes 17301504 | tf_op jit(solution)/shard_map/reduce_scatter | solution.py:196
  (25 other events, 84.4 us)
Sparse Core Ops, SparseCore 0:
  10.9 69.8 all-gather.6
  135.5 53.8 all-gather.8
  192.3 55.7 all-gather.10
  250.8 83.0 all-gather.12
  336.6 80.6 all-gather.14
  554.2 321.3 reduce-scatter.5
  878.6 125.1 reduce-scatter.9
  1011.4 172.6 reduce-scatter.7
  1187.0 184.4 reduce-scatter.13
  1374.2 184.4 reduce-scatter.11
where the time goes:
time: 1580 us; the launch traced here: 1570 us
  waiting for transfers between devices  963 us (61%)
  blocking collectives  276 us (17%)
  local copies, waits for them, and re-layouts  122 us (8%)
  matrix products  118 us (7%)
  loops' own time  32.7 us (2%)
  other arithmetic  29.2 us (2%)
    reduce_scatter x1, waiting for transfers between devices, on_device(): lax.psum_scatter(grad_pairs.reshape(block_rows * n_blk, 2, group_width).a...  316 us
    reduce_scatter x1, waiting for transfers between devices, on_device(): lax.psum_scatter(down_weight_grad, ('head', 'blk'), scatter_dimension=0,...  187 us
    reduce_scatter x1, waiting for transfers between devices, on_device(): lax.psum_scatter(up_weight_grad, ('head', 'blk'), scatter_dimension=0, ti...  187 us
    reduce_scatter x1, waiting for transfers between devices, on_device(): lax.psum_scatter(in_weight_grad, ('head', 'blk'), scatter_dimension=0, ti...  146 us
    all_gather x1, blocking collectives, on_device(): lax.all_gather(up_bias, ('head', 'blk'), axis=0, tiled=True)  95.4 us
    unnamed x2, blocking collectives  82.6 us
    all_to_all x1, blocking collectives, on_device(): lax.all_to_all(grad_joint.reshape(block_rows, 3, 1, group_width), 'head',...  59.2 us
    all_gather x1, waiting for transfers between devices, on_device(): piece = lax.all_gather(kv_local, 'blk', axis=0, tiled=True)  50.8 us
  transfers between devices with their start and end apart: 12, of which 8 were waited for; matrix products, arithmetic and copies ran while one was open for 9% of the time, Pallas kernels for 0%

commit v1 on v0

--- a/solution.py
+++ b/solution.py
@@ -8,6 +8,15 @@
 EPS = 1e-05
 NEGATIVE = -1e30
 GELU_C = 0.7978845608028654
+
+
+def leaves_lead(here_x, join_dim, out_dim=2):
+    met_up = lax.axis_size("head")
+    y1 = jnp.split(here_x, met_up, join_dim)
+    local_part = jnp.stack(y1, 0)
+    v1 = lax.all_to_all(local_part, concat_axis=0, axis_name="head", split_axis=0)
+    extra = jnp.concatenate(v1, out_dim)
+    return extra
 
 
 def norm_forward(rows, gain, shift):
@@ -264,13 +273,7 @@
         [grad_query.reshape(block_rows, 1, group_width).astype(bf16), pair_sums.astype(bf16)],
         axis=1,
     )
-    grad_rows = lax.all_to_all(
-        grad_joint.reshape(block_rows, 3, 1, group_width),
-        "head",
-        split_axis=0,
-        concat_axis=2,
-        tiled=True,
-    )
+    grad_rows = leaves_lead(grad_joint.reshape(block_rows, 3, 1, group_width), 0)
     grad_proj = grad_rows.reshape(tok_rows, 3 * width)
     query_bias_grad = jnp.sum(grad_proj[:, :width].astype(f32), axis=0)
     value_bias_grad = jnp.sum(grad_proj[:, 2 * width :].astype(f32), axis=0)

time: 1580 us -> 1580 us (level)
  waiting for transfers between devices: 963 us -> 984 us
    reduce_scatter x1, waiting for transfers between devices: 146 us -> 167 us  [on_device(): lax.psum_scatter(in_weight_grad, ('head', 'blk'), scatter_dimension=0, ti...]
    unnamed x103 -> x105, local copies, waits for them, and re-layouts: 32.6 us -> 34 us
where the time goes in v1:
time: 1580 us; the launch traced here: 1560 us
  waiting for transfers between devices  984 us (62%)
  blocking collectives  262 us (17%)
  matrix products  117 us (7%)
  local copies, waits for them, and re-layouts  115 us (7%)
  loops' own time  32.9 us (2%)
  other arithmetic  28.2 us (2%)
    reduce_scatter x1, waiting for transfers between devices, on_device(): lax.psum_scatter(grad_pairs.reshape(block_rows * n_blk, 2, group_width).a...  316 us
    reduce_scatter x1, waiting for transfers between devices, on_device(): lax.psum_scatter(down_weight_grad, ('head', 'blk'), scatter_dimension=0,...  187 us
    reduce_scatter x1, waiting for transfers between devices, on_device(): lax.psum_scatter(up_weight_grad, ('head', 'blk'), scatter_dimension=0, ti...  187 us
    reduce_scatter x1, waiting for transfers between devices, on_device(): lax.psum_scatter(in_weight_grad, ('head', 'blk'), scatter_dimension=0, ti...  167 us
    all_gather x1, blocking collectives, on_device(): lax.all_gather(up_bias, ('head', 'blk'), axis=0, tiled=True)  95.2 us
    unnamed x2, blocking collectives  82.5 us
    all_gather x1, waiting for transfers between devices, on_device(): piece = lax.all_gather(kv_local, 'blk', axis=0, tiled=True)  50.8 us
    all_to_all x1, blocking collectives, leaves_lead(): lax.all_to_all(local_part, concat_axis=0, axis_name='head', split_axis=0)  45.7 us
  transfers between devices with their start and end apart: 12, of which 8 were waited for; matrix products, arithmetic and copies ran while one was open for 9% of the time, Pallas kernels for 0%

profile of v1, /device:TPU:14, one launch (start us, length us, event | category | flops | bytes accessed | tf_op | source)
XLA Modules:
  0.0 1564.3 jit_solution(10832903660457688252)
XLA Ops:
  14.7 41.5 %all-reduce.18 = (bf16[1024]{0:T(1024)(128)(2,1)S(1)}, bf16[1024]{0:T(1024)(128)(2,1)S(1)}, bf16[1024]{0:T(1024)(128)(2,1)S(1)}, bf16[1024]{0:T(1024)(128)(2,1)S...) all-reduce(bf16[1024]{0:T(1024)(128)(2,1)S(1)} %dynamic-update-slic, ...), channel_id=1, replica_groups=mesh['head'=4,'blk'=8] {'head','blk'}, use_global_device_ids=true, to_apply=%add.3 | all-reduce | flops 8192 | bytes 32768
  59.0 21.8 %all-gather.7.cloned.1.call-done = bf16[1024,3072]{1,0:T(8,128)(2,1)} async-done(((bf16[32,3072]{1,0:T(8,128)(2,1)}), bf16[1024,3072]{1,0:T(8,128)(2,1)}) %all-gather.7.cloned.1.call-update) | async-done | bytes 6291472 | tf_op jit(solution)/shard_map/all_gather | solution.py:83
  90.3 39.0 %all_to_all.50 = bf16[256,3,4,256]{3,0,1,2:T(8,128)(2,1)S(1)} all-to-all(bf16[256,3,4,256]{3,0,1,2:T(8,128)(2,1)S(1)} %copy.95), channel_id=1, replica_groups=mesh['head'=4,'blk'=8] {'head'}, dimensions={2} | all-to-all | bytes 3145728 | tf_op jit(solution)/shard_map/all_to_all | solution.py:94
  138.6 50.8 %all-gather.9.cloned.1.call-done = bf16[8192,2,256]{0,2,1:T(8,128)(2,1)} async-done(((bf16[1024,2,256]{0,2,1:T(8,128)(2,1)}), bf16[8192,2,256]{0,2,1:T(8,128)(2,1)}) %all-gather.9.cloned.1.call-update) | async-done | bytes 8388624 | tf_op jit(solution)/shard_map/all_gather | solution.py:130
  189.4 12.0 copy.97
  201.4 11.5 copy.98
  213.1 45.0 %while.38 = (s32[]{:T(128)}, f32[1024,4,64]{0,2,1:T(8,128)S(1)}, f32[4,1024]{1,0:T(4,128)S(1)}, f32[4,1024]{1,0:T(4,128)S(1)}, s32[8]{0:T(128)S(1)}, /*index=5*/...) while((s32[]{:T(128)}, f32[1024,4,64]{0,2,1:T(8,128)S(1)}, ...), condition=%wide.region_7.8_spmd.clone, body=%wide.region_2.7_spmd.clone.sunk | while | flops 1123563520 | bytes 60596688 | solution.py:153
  240.2 13.9 conditional.6
  266.1 95.2 %all-gather = bf16[32,1,128]{2,1,0:T(2,128)(2,1)S(1)} all-gather(bf16[1,1,128]{2,1,0:T(2,128)(2,1)S(1)} %bitcast.165), channel_id=1, replica_groups=mesh['head'=4,'blk'=8] {'head','blk'}, dimensions={0}, use_global_device_ids=true | all-gather | bytes 8448 | tf_op jit(solution)/shard_map/all_gather | solution.py:172
  377.6 39.7 %all-gather.15.cloned.1.call-done = bf16[4096,1024]{1,0:T(8,128)(2,1)} async-done(((bf16[128,1024]{1,0:T(8,128)(2,1)}), bf16[4096,1024]{1,0:T(8,128)(2,1)}) %all-gather.15.cloned.1.call-update) | async-done | bytes 8388624 | tf_op jit(solution)/shard_map/all_gather | solution.py:173
  417.3 11.8 convert_reduce_fusion
  440.0 12.0 all-to-all-done.2
  463.6 81.6 %while.39 = (s32[]{:T(128)}, f32[1024,4,64]{0,2,1:T(8,128)}, f32[8192,2,4,64]{0,3,2,1:T(8,128)}, s32[8]{0:T(128)S(1)}, s32[]{:T(128)}, /*index=5*/s32[8192]{0:T(...) while((s32[]{:T(128)}, f32[1024,4,64]{0,2,1:T(8,128)}, ...), condition=%wide.region_16.17_spmd.clone, body=%wide.region_13.16_spmd.clone.sunk | while | flops 2731280384 | bytes 103375360 | solution.py:264
  491.2 50.0 %conditional.7 = ((f32[1024,4,64]{0,2,1:T(8,128)}, f32[8192,2,4,64]{0,3,2,1:T(8,128)})) conditional(s32[]{:T(128)} %convert_element_type.245, (f32[1024,4,64]{0,2,1:T(8,128)}, f32[8192,2,4,64]{0,3,2,1:T(8,128)}) %tuple.146, (s32[]{:T(128)}, s32[]{:T(128)}, s32[8192]{0:T(1024)}, s32[1024]{0:T(1024)S(1)}, bf16[8,1024,2,256]{1,3,2,0:T(8,128)(2,1)}, ...), branch_computations={%region_14.14_spmd, %region_15.15_spmd} | conditional | flops 2731280384 | bytes 103370856 | solution.py:262
  502.6 10.3 fusion.27
  530.9 10.3 dynamic_update_slice.3
  559.6 316.4 %reduce-scatter.6.cloned.1.call-done = bf16[1024,2,256]{0,2,1:T(8,128)(2,1)} async-done(((bf16[8192,2,256]{0,2,1:T(8,128)(2,1)}), bf16[1024,2,256]{0,2,1:T(8,128)(2,1)}) %reduce-scatter.6.cloned.1.call-update) | async-done | bytes 1048592 | tf_op jit(solution)/shard_map/reduce_scatter | solution.py:266
  877.6 45.7 %all_to_all.51 = bf16[4,256,3,1,256]{1,4,2,3,0:T(8,128)(2,1)S(1)} all-to-all(bf16[4,256,3,1,256]{1,4,2,3,0:T(8,128)(2,1)S(1)} %pad_maximum_fusion), channel_id=1, replica_groups=mesh['head'=4,'blk'=8] {'head'}, dimensions={0} | all-to-all | bytes 3145728 | tf_op jit(solution)/shard_map/all_to_all | solution.py:17
  932.1 10.8 fusion.77
  944.2 9.8 fusion.76
  968.5 41.0 %all-reduce.17 = (f32[1024]{0:T(1024)S(1)}, f32[1024]{0:T(1024)S(1)}, f32[1024]{0:T(1024)S(1)}, f32[1024]{0:T(1024)S(1)}, f32[1024]{0:T(1024)S(1)}, /*index=5*/f...) all-reduce(f32[1024]{0:T(1024)S(1)} %get-tuple-element.973, ...), channel_id=3, replica_groups=mesh['head'=4,'blk'=8] {'head','blk'}, use_global_device_ids=true, to_apply=%region_21.22.clone | all-reduce | flops 12288 | bytes 98304
  1016.0 166.6 %reduce-scatter.8.cloned.1.call-done = f32[32,3072]{1,0:T(8,128)} async-done(((f32[1024,3072]{1,0:T(8,128)}), f32[32,3072]{1,0:T(8,128)}) %reduce-scatter.8.cloned.1.call-update) | async-done | bytes 393232 | tf_op jit(solution)/shard_map/reduce_scatter | solution.py:297
  1182.6 187.4 %reduce-scatter.14.cloned.1.call-done = f32[128,1024]{1,0:T(8,128)} async-done(((f32[4096,1024]{1,0:T(8,128)}), f32[128,1024]{1,0:T(8,128)}) %reduce-scatter.14.cloned.1.call-update) | async-done | bytes 524304 | tf_op jit(solution)/shard_map/reduce_scatter | solution.py:207
  1370.0 187.2 %reduce-scatter.12.cloned.1.call-done = f32[32,4096]{1,0:T(8,128)} async-done(((f32[1024,4096]{1,0:T(8,128)}), f32[32,4096]{1,0:T(8,128)}) %reduce-scatter.12.cloned.1.call-update) | async-done | bytes 524304 | tf_op jit(solution)/shard_map/reduce_scatter | solution.py:205
  (272 shorter events, 195.7 us)
Async XLA Ops:
  7.2 73.5 %all-gather.7.cloned.1.call-start = ((), (), s32[]{:S(2)}) async-start(), calls=%async_computation.9 | async-start | bytes 6488064 | tf_op jit(solution)/shard_map/all_gather | solution.py:83
  7.9 181.5 %all-gather.9.cloned.1.call-start = ((), (), s32[]{:S(2)}) async-start(), calls=%async_computation.10 | async-start | bytes 9437184 | tf_op jit(solution)/shard_map/all_gather | solution.py:130
  135.4 231.0 %all-gather.11.cloned.1.call-start = ((), (), s32[]{:S(2)}) async-start(), calls=%async_computation.11 | async-start | bytes 2162688 | tf_op jit(solution)/shard_map/all_gather | solution.py:86
  136.2 233.4 %all-gather.13.cloned.1.call-start = ((), (), s32[]{:S(2)}) async-start(), calls=%async_computation.12 | async-start | bytes 8650752 | tf_op jit(solution)/shard_map/all_gather | solution.py:171
  136.8 280.6 %all-gather.15.cloned.1.call-start = ((), (), s32[]{:S(2)}) async-start(), calls=%async_computation.13 | async-start | bytes 8650752 | tf_op jit(solution)/shard_map/all_gather | solution.py:173
  258.7 107.8 %copy-start.5 = (bf16[256,1024]{1,0:T(8,128)(2,1)S(1)}, bf16[256,1024]{1,0:T(8,128)(2,1)}, u32[]{:S(2)}) copy-start(bf16[256,1024]{1,0:T(8,128)(2,1)} %param.24) | copy-start | bytes 1572868
  260.9 100.4 %all-to-all-start.1 = ((bf16[4,2,32768]{2,1,0:T(2,128)(2,1)}), bf16[4,2,32768]{2,1,0:T(2,128)(2,1)}, u32[]{:S(2)}, u32[]{:S(2)}) async-start(bf16[4,2,32768]{2,1,0:T(2,128)(2,1)} %reshape.315), calls=%async_computation.1 | async-start | bytes 1048576 | tf_op jit(solution)/shard_map/all_to_all | solution.py:158
  266.0 166.3 %copy-start.14 = (f32[1024]{0:T(1024)}, f32[1024]{0:T(1024)S(1)}, u32[]{:S(2)}) copy-start(f32[1024]{0:T(1024)S(1)} %convert_element_type.143) | copy-start | bytes 12292
  266.0 103.5 %copy-start.16 = (f32[1024]{0:T(1024)}, f32[1024]{0:T(1024)S(1)}, u32[]{:S(2)}) copy-start(f32[1024]{0:T(1024)S(1)} %convert_element_type.144) | copy-start | bytes 12292
  369.2 63.1 %copy-start.1 = (f32[256,1024]{1,0:T(8,128)}, f32[256,1024]{1,0:T(8,128)S(1)}, u32[]{:S(2)}) copy-start(f32[256,1024]{1,0:T(8,128)S(1)} %get-tuple-element.1066) | copy-start | bytes 3145732
  369.3 63.1 %copy-start.22 = (f32[256]{0:T(256)}, f32[256]{0:T(256)S(1)}, u32[]{:S(2)}) copy-start(f32[256]{0:T(256)S(1)} %broadcast_multiply_fusion.4) | copy-start | bytes 3076
  369.5 62.9 %copy-start.26 = (f32[256]{0:T(256)}, f32[256]{0:T(256)S(1)}, u32[]{:S(2)}) copy-start(f32[256]{0:T(256)S(1)} %add_rsqrt_fusion) | copy-start | bytes 3076
  369.6 47.7 %copy-start.11 = (bf16[256,1024]{1,0:T(8,128)(2,1)S(1)}, bf16[256,1024]{1,0:T(8,128)(2,1)}, u32[]{:S(2)}) copy-start(bf16[256,1024]{1,0:T(8,128)(2,1)} %param.25) | copy-start | bytes 1572868
  436.0 15.9 %all-to-all-start.2 = ((bf16[256,4,256]{2,0,1:T(8,128)(2,1)}), bf16[256,4,256]{2,0,1:T(8,128)(2,1)S(1)}, u32[]{:S(2)}, u32[]{:S(2)}) async-start(bf16[256,4,256]{2,0,1:T(8,128)(2,1)} %bitcast.133), calls=%async_computation.2 | async-start | bytes 1048576 | tf_op jit(solution)/shard_map/all_to_all | solution.py:214
  440.0 436.0 %reduce-scatter.6.cloned.1.call-start = ((), (), s32[]{:S(2)}) async-start(), calls=%async_computation.14 | async-start | bytes 9437184 | tf_op jit(solution)/shard_map/reduce_scatter | solution.py:266
  554.2 461.8 %reduce-scatter.10.cloned.1.call-start = ((), (), s32[]{:S(2)}) async-start(), calls=%async_computation.16 | async-start | bytes 4325376 | tf_op jit(solution)/shard_map/reduce_scatter | solution.py:300
  558.3 624.4 %reduce-scatter.8.cloned.1.call-start = ((), (), s32[]{:S(2)}) async-start(), calls=%async_computation.15 | async-start | bytes 12976128 | tf_op jit(solution)/shard_map/reduce_scatter | solution.py:297
  877.3 47.2 %copy-start.6 = (bf16[256,1024]{1,0:T(8,128)(2,1)S(1)}, bf16[256,1024]{1,0:T(8,128)(2,1)}, u32[]{:S(2)}) copy-start(bf16[256,1024]{1,0:T(8,128)(2,1)} %param.24) | copy-start | bytes 1572868
  877.3 47.2 %copy-start.19 = (f32[1024]{0:T(1024)S(1)}, f32[1024]{0:T(1024)}, u32[]{:S(2)}) copy-start(f32[1024]{0:T(1024)} %copy-done.18) | copy-start | bytes 12292
  877.3 47.2 %copy-start.21 = (f32[1024]{0:T(1024)S(1)}, f32[1024]{0:T(1024)}, u32[]{:S(2)}) copy-start(f32[1024]{0:T(1024)} %copy-done.20) | copy-start | bytes 12292
  877.3 47.2 %copy-start.25 = (f32[256]{0:T(256)S(1)}, f32[256]{0:T(256)}, u32[]{:S(2)}) copy-start(f32[256]{0:T(256)} %copy-done.24) | copy-start | bytes 3076
  877.4 47.2 %copy-start.29 = (f32[256]{0:T(256)S(1)}, f32[256]{0:T(256)}, u32[]{:S(2)}) copy-start(f32[256]{0:T(256)} %copy-done.28) | copy-start | bytes 3076
  931.1 438.9 %reduce-scatter.14.cloned.1.call-start = ((), (), s32[]{:S(2)}) async-start(), calls=%async_computation.18 | async-start | bytes 17301504 | tf_op jit(solution)/shard_map/reduce_scatter | solution.py:207
  943.0 614.3 %reduce-scatter.12.cloned.1.call-start = ((), (), s32[]{:S(2)}) async-start(), calls=%async_computation.17 | async-start | bytes 17301504 | tf_op jit(solution)/shard_map/reduce_scatter | solution.py:205
  (26 other events, 195.8 us)
Sparse Core Ops, SparseCore 0:
  10.9 69.8 all-gather.6
  135.6 53.8 all-gather.8
  192.3 55.6 all-gather.10
  250.7 83.0 all-gather.12
  336.6 80.6 all-gather.14
  554.4 321.5 reduce-scatter.5
  878.9 119.9 reduce-scatter.9
  1006.6 176.0 reduce-scatter.7
  1185.5 184.4 reduce-scatter.13
  1372.7 184.4 reduce-scatter.11
